TPU v7x, 256 devices: a whole 4x4x8 slice. The times are simulated.
256 devices in a mesh: req: 2 (over core), row: 32 (over x, z), col: 4 (over y).
Axes of the slice: x: 4, y: 4, z: 8, core: 2. Of those that a mesh axis runs over, the one named last changes fastest.
Arguments:
- hidden: bfloat16 [2, 3072, 3072], P('req', 'row'), may hold values from -6 to 6
- text_hidden: bfloat16 [2, 128, 3072], P('req', 'row'), may hold values from -6 to 6
- text_len: int32 [2], replicated, may hold values from 32 to 128, as said below
- grid: int32 [2, 2], replicated, may hold values from 8 to 32, as said below
- timestep: int32 [2], replicated, may hold values from 250 to 999
- modulation: float32 [2, 8, 3072], P('req'), may hold values from -4 to 4
- q_gain: float32 [64], replicated, may hold values from 1 to 3
- k_gain: float32 [64], replicated, may hold values from 1 to 3
- w_qkv: bfloat16 [3, 3072, 3072], P(None, 'row', 'col'), may hold values from -0.109375 to 0.109375
- w_out: bfloat16 [3072, 3072], P('col'), may hold values from -0.109375 to 0.109375
- w_up: bfloat16 [3072, 12288], P(None, 'row'), may hold values from -0.109375 to 0.109375
- w_down: bfloat16 [12288, 3072], P('row'), may hold values from -0.0546875 to 0.0546875
- w_proj: bfloat16 [3072, 64], replicated, may hold values from -0.109375 to 0.109375
- latent: float32 [2, 3072, 64], P('req', ('row', 'col')), may hold values from -6 to 6
- conv_w: bfloat16 [3, 3, 16, 512], replicated, may hold values from -0.5 to 0.5
Outputs:
- hidden_out: bfloat16 [2, 3072, 3072], P('req', ('row', 'col'))
- new_latent: float32 [2, 3072, 64], P('req', ('row', 'col'))
- decoded: bfloat16 [2, 6, 64, 32, 512], P('req', None, 'row', 'col')
Inputs may be any that keep to these rules, and one draw needn't show every extreme that they name: Each request's live token rows and columns; one of the two requests, drawn, fills its whole grid of 32 rows and 16 columns, the other keeps at least half of each. `text_len`: one of the two requests, drawn, has all 128 text tokens live. The previous timestep of the sampling step is timestep - 250.
All inputs are finite; a program needn't handle non-finite values.
Results may differ from a plain program's by a relative error of at most 0.014.
Values may be sent and summed in bfloat16 or wider, within the bound.
A program may use at most 128 MiB of HBM per device.

v0:
```python
import jax
import jax.numpy as jnp
from jax import lax
from jax.sharding import PartitionSpec as P

CH = 16
FR = 6
TR = 1
TC = 4
TRAIN_STEPS = 1000
STRIDE = 250
latent_scale = 0.7


def extended(cells, sides, width):
    for axis, dim in sides:
        count = lax.axis_size(axis)
        ends = count - 1
        head = lax.slice_in_dim(cells, 0, width, axis=dim)
        tail = lax.slice_in_dim(cells, cells.shape[dim] - width, cells.shape[dim], axis=dim)
        cells = jnp.concatenate(
            [
                lax.ppermute(tail, axis, [(i, (i + 1) % count) for i in range(ends)]),
                cells,
                lax.ppermute(head, axis, [((i + 1) % count, i) for i in range(ends)]),
            ],
            axis=dim,
        )
    return cells


def layer_norm(tensor, epsilon):
    average = jnp.mean(tensor, axis=-1, keepdims=True)
    centered = tensor - average
    spread = jnp.mean(centered * centered, axis=-1, keepdims=True)
    return centered * lax.rsqrt(spread + epsilon)


def modulate(tensor, offset, factor):
    return (layer_norm(tensor, 1e-05) * (1.0 + factor) + offset).astype(jnp.bfloat16)


def head_norm(tensor, scaling):
    return (layer_norm(tensor, 1e-06) * scaling).astype(jnp.bfloat16)


def pick_entry(entries, position):
    slot_ids = jnp.arange(entries.shape[0], dtype=jnp.int32)
    return jnp.sum(jnp.where(slot_ids == position, entries, jnp.zeros_like(entries)))


def solver_weights(step_index):
    plan = jnp.linspace(0.00085**0.5, 0.012**0.5, TRAIN_STEPS, dtype=jnp.float32) ** 2
    cumulative = jnp.cumprod(1.0 - plan)
    alpha_now = pick_entry(cumulative, step_index)
    alpha_prev = pick_entry(cumulative, step_index - STRIDE)
    root_now = jnp.sqrt(alpha_now)
    rest_now = jnp.sqrt(1.0 - alpha_now)
    root_prev = jnp.sqrt(alpha_prev)
    rest_prev = jnp.sqrt(1.0 - alpha_prev)
    return (
        root_prev * root_now + rest_prev * rest_now,
        rest_prev * root_now - root_prev * rest_now,
    )


def key_mask(count, owners, grid, text_len, span, block_tokens, tile, text_rows):
    positions = jnp.arange(count, dtype=jnp.int32)
    owner_row = positions // span
    within = positions % span
    is_video = within < block_tokens
    owner_col = within // tile
    local_ids = within % tile
    token_row = owner_row * TR + local_ids // TC % TR
    token_col = owner_col * TC + local_ids % TC
    text_index = owner_row * text_rows + within - block_tokens
    matches = jnp.arange(grid.shape[0], dtype=jnp.int32)[None, :] == owners[:, None]
    rows_live = jnp.sum(jnp.where(matches, grid[None, :, 0], 0), axis=1)
    cols_live = jnp.sum(jnp.where(matches, grid[None, :, 1], 0), axis=1)
    text_lens = jnp.sum(jnp.where(matches, text_len[None, :], 0), axis=1)
    video_live = (token_row[None, :] < rows_live[:, None]) & (
        token_col[None, :] < cols_live[:, None]
    )
    text_live = text_index[None, :] < text_lens[:, None]
    return jnp.where(is_video[None, :], video_live, text_live).astype(jnp.float32)


def projector(stacked, piece):
    return jnp.einsum("gld,cde->cgle", stacked, piece, preferred_element_type=jnp.float32)


def attention_step(queries, owners, grid, text_len, span, block_tokens, tile, text_rows):
    score_scale = queries.shape[3] ** (-0.5)

    def attend(carry, pieces, start):
        key_piece, value_piece = pieces
        live_keys = key_mask(
            key_piece.shape[1], owners, grid, text_len, span, block_tokens, tile, text_rows
        )
        scores = (
            jnp.einsum("gqhd,gkhd->gqhk", queries, key_piece, preferred_element_type=jnp.float32)
            * score_scale
        )
        raw_weights = jnp.exp(scores) * live_keys[:, None, None, :]
        weighted = jnp.einsum(
            "gqhk,gkhd->gqhd",
            raw_weights.astype(jnp.bfloat16),
            value_piece,
            preferred_element_type=jnp.float32,
        )
        return (weighted, jnp.sum(raw_weights, axis=3))

    return attend


def shards(
    hidden,
    text_hidden,
    text_len,
    grid,
    timestep,
    modulation,
    q_gain,
    k_gain,
    w_qkv,
    w_out,
    w_up,
    w_down,
    w_proj,
    latent,
    conv_w,
):
    col_count = lax.axis_size("col")
    request_id = lax.axis_index("req")
    row_id = lax.axis_index("row")
    col_id = lax.axis_index("col")
    block_tokens = hidden.shape[1]
    tile = block_tokens // col_count
    text_rows = text_hidden.shape[1]
    head_dim = q_gain.shape[0]
    adaptive = modulation[0]
    source = hidden[0].astype(jnp.float32)
    joined = jnp.concatenate(
        [
            modulate(source, adaptive[0], adaptive[1]),
            modulate(text_hidden[0].astype(jnp.float32), adaptive[0], adaptive[1]),
        ],
        axis=0,
    )
    span = joined.shape[0]
    stacked = joined[None]
    owners = jnp.reshape(request_id, (1,))
    half_cols = w_qkv.shape[2] // 2
    own_half = lax.dynamic_slice_in_dim(w_qkv, request_id * half_cols, half_cols, 2)
    gathered_half = lax.all_gather(own_half, "row", axis=1, tiled=True)
    qkv = projector(stacked, lax.all_gather(gathered_half, "req", axis=2, tiled=True))
    groups = stacked.shape[0]
    heads_here = qkv.shape[3] // head_dim
    shaped = qkv.reshape(3, groups, span, heads_here, head_dim)
    queries = head_norm(shaped[0, :, :block_tokens], q_gain)
    key_block = head_norm(shaped[1], k_gain)
    value_block = shaped[2].astype(jnp.bfloat16)
    attend = attention_step(queries, owners, grid, text_len, span, block_tokens, tile, text_rows)
    empty_state = (jnp.zeros(queries.shape, jnp.float32), jnp.zeros(queries.shape[:3], jnp.float32))
    both = jnp.stack([key_block[0], value_block[0]], axis=0)[None]
    both = lax.all_gather(both, "row", axis=0, tiled=True)
    both = jnp.swapaxes(both, 0, 1).reshape(2, 1, -1, heads_here, head_dim)
    weighted, totals = attend(empty_state, (both[0], both[1]), jnp.int32(0))
    attended = (
        (weighted / totals[..., None])
        .astype(jnp.bfloat16)
        .reshape(groups * block_tokens, heads_here * head_dim)
    )
    partial_out = jnp.dot(attended, w_out, preferred_element_type=jnp.float32)
    projected = lax.psum_scatter(partial_out, "col", scatter_dimension=0, tiled=True)
    own_rows = lax.dynamic_slice_in_dim(source, col_id * tile, tile, 0)
    mixed = lax.optimization_barrier(
        (own_rows + adaptive[2] * projected).astype(jnp.bfloat16)
    ).astype(jnp.float32)
    second_norm = modulate(mixed, adaptive[3], adaptive[4])
    hidden_units = jax.nn.gelu(
        jnp.dot(
            lax.all_gather(second_norm, "row", axis=0, tiled=True),
            w_up,
            preferred_element_type=jnp.float32,
        ),
        approximate=True,
    ).astype(jnp.bfloat16)
    feed_terms = jnp.dot(hidden_units, w_down, preferred_element_type=jnp.float32)
    feed_out = lax.psum_scatter(
        feed_terms.astype(jnp.bfloat16), "row", scatter_dimension=0, tiled=True
    ).astype(jnp.float32)
    out_hidden = (mixed + adaptive[5] * feed_out).astype(jnp.bfloat16)
    final_norm = modulate(out_hidden.astype(jnp.float32), adaptive[6], adaptive[7])
    velocity = jnp.dot(final_norm, w_proj, preferred_element_type=jnp.float32)
    local_ids = jnp.arange(tile, dtype=jnp.int32)
    token_row = row_id * TR + local_ids // TC % TR
    token_col = col_id * TC + local_ids % TC
    rows_live = pick_entry(grid[:, 0], request_id)
    cols_live = pick_entry(grid[:, 1], request_id)
    live_tokens = ((token_row < rows_live) & (token_col < cols_live)).astype(jnp.float32)
    keep_part, velocity_part = solver_weights(pick_entry(timestep, request_id))
    updated = (keep_part * latent[0] + velocity_part * velocity) * live_tokens[:, None]
    pixels = (
        updated.reshape(FR, TR, TC, CH, 2, 2)
        .transpose(0, 1, 4, 2, 5, 3)
        .reshape(FR, 2 * TR, 2 * TC, CH)
    )
    scaled = (pixels / latent_scale).astype(jnp.bfloat16)
    padded = extended(scaled, (("row", 1), ("col", 2)), 1)
    running = jnp.zeros((FR, 2 * TR, 2 * TC, conv_w.shape[3]), jnp.float32)
    for row_tap in range(3):
        for col_tap in range(3):
            window = padded[:, row_tap : row_tap + 2 * TR, col_tap : col_tap + 2 * TC, :]
            running = running + jnp.einsum(
                "fyxc,cd->fyxd",
                window,
                conv_w[row_tap, col_tap],
                preferred_element_type=jnp.float32,
            )
    return (out_hidden[None], updated[None], running.astype(jnp.bfloat16)[None])


def solution(mesh):
    placed = (
        P("req", "row", None),
        P("req", "row", None),
        P(),
        P(),
        P(),
        P("req", None, None),
        P(),
        P(),
        P(None, "row", "col"),
        P("col", None),
        P(None, "row"),
        P("row", None),
        P(),
        P("req", ("row", "col"), None),
        P(),
    )
    return jax.shard_map(
        shards,
        mesh=mesh,
        in_specs=placed,
        out_specs=(
            P("req", ("row", "col"), None),
            P("req", ("row", "col"), None),
            P("req", None, "row", "col", None),
        ),
        check_vma=False,
    )
```

profile of v0, /device:TPU:26, one launch (start us, length us, event | category | flops | bytes accessed | tf_op | source)
XLA Modules:
  0.0 706.1 jit_solution(1297304816965305826)
XLA Ops:
  7.2 1.8 constant_dynamic-slice_fusion
  9.1 95.0 %all-gather.6.cloned.1.call-done = bf16[3,3072,384]{2,1,0:T(8,128)(2,1)} async-done(((bf16[3,96,384]{2,1,0:T(8,128)(2,1)}), bf16[3,3072,384]{2,1,0:T(8,128)(2,1)}) %all-gather.6.cloned.1.call-update) | async-done | bytes 7077904 | tf_op jit(solution)/shard_map/all_gather | solution.py:155
  107.4 28.7 %all-gather.8.cloned.1.call-done = bf16[3,3072,768]{2,1,0:T(8,128)(2,1)} async-done(((bf16[3,3072,384]{2,1,0:T(8,128)(2,1)}), bf16[3,3072,768]{2,1,0:T(8,128)(2,1)}) %all-gather.8.cloned.1.call-update) | async-done | bytes 14155792 | tf_op jit(solution)/shard_map/all_gather | solution.py:156
  136.1 7.0 convolution_bitcast_fusion
  143.2 0.9 copy-done.4
  144.8 0.8 pad_maximum_fusion
  147.3 2.0 fusion.152
  149.3 1.6 copy.32
  152.3 113.2 %all-gather.12.cloned.1.call-done = bf16[64,100,12,64]{1,3,2,0:T(8,128)(2,1)} async-done(((bf16[2,100,12,64]{1,3,2,0:T(8,128)(2,1)}), bf16[64,100,12,64]{1,3,2,0:T(8,128)(2,1)}) %all-gather.12.cloned.1.call-update) | async-done | bytes 9830416 | tf_op jit(solution)/shard_map/all_gather | solution.py:166
  265.5 11.9 %copy.45 = bf16[32,2,100,12,64]{2,0,4,3,1:T(8,128)(2,1)S(1)} copy(bf16[32,2,100,12,64]{2,4,3,1,0:T(8,128)(2,1)} %bitcast.213) | data formatting | bytes 19660800 | tf_op jit(solution)/shard_map/all_gather | solution.py:166
  277.4 5.5 fusion.175
  282.9 12.9 %reshape.413 = bf16[3200,12,64]{0,2,1:T(8,128)(2,1)} reshape(bf16[1,32,100,12,64]{2,1,4,3,0:T(8,128)(2,1)} %get-tuple-element.10) | data formatting | bytes 9830400 | tf_op jit(solution)/shard_map/reshape.45
  295.8 13.0 %reshape.414 = bf16[3200,12,64]{0,2,1:T(8,128)(2,1)} reshape(bf16[1,32,100,12,64]{2,1,4,3,0:T(8,128)(2,1)} %get-tuple-element.9) | data formatting | bytes 9830400 | tf_op jit(solution)/shard_map/reshape.37
  308.7 10.7 %bitcast_reduce_fusion = (f32[96,12]{0,1:T(8,128)S(1)}, f32[12,3200,96]{1,2,0:T(8,128)}) fusion(f32[3200]{0:T(1024)S(1)} %fusion.152, bf16[3200,12,64]{0,2,1:T(8,128)(2,1)} %reshape.414, f32[3,1,100,12,64]{2,4,3,0,1:T(8,128)} %bitcast.219, f32[64]{0:T(128)S(1)} %copy-done.23, f32[96,12]{0,1:T(8,128)S(1)} %copy-done.15, f32[96,12]{0,1:T(8,128)S(1)} %copy-done.10), kind=kOutput, calls=%fused_computation | convolution fusion | flops 483212160 | bytes 20080896 | tf_op jit(solution)/shard_map/gqhd,gkhd->gqhk/dot_general | solution.py:101
  319.4 8.3 %fusion.29 = bf16[1,96,12,64]{1,3,2,0:T(8,128)(2,1)S(1)} fusion(bf16[3200,12,64]{0,2,1:T(8,128)(2,1)S(1)} %bitcast.212, f32[12,3200,96]{1,2,0:T(8,128)} %get-tuple-element.24, f32[3200]{0:T(1024)S(1)} %fusion.152, f32[96,12]{0,1:T(8,128)S(1)} %get-tuple-element.23), kind=kOutput, calls=%fused_computation.37 | convolution fusion | flops 483065856 | bytes 19825664 | tf_op jit(solution)/shard_map/gqhk,gkhd->gqhd/dot_general | solution.py:105
  327.7 4.4 fusion.179
  332.2 1.1 convert_element_type.114
  333.3 22.0 %reduce-scatter.3.cloned.1.call-done = f32[24,3072]{1,0:T(8,128)} async-done(((f32[96,3072]{1,0:T(8,128)}), f32[24,3072]{1,0:T(8,128)}) %reduce-scatter.3.cloned.1.call-update) | async-done | bytes 294928 | tf_op jit(solution)/shard_map/reduce_scatter | solution.py:175
  355.3 1.1 fusion.57
  357.9 84.8 %all-gather.10.cloned.1.call-done = bf16[768,3072]{1,0:T(8,128)(2,1)} async-done(((bf16[24,3072]{1,0:T(8,128)(2,1)}), bf16[768,3072]{1,0:T(8,128)(2,1)}) %all-gather.10.cloned.1.call-update) | async-done | bytes 4718608 | tf_op jit(solution)/shard_map/all_gather | solution.py:183
  442.7 10.4 %convolution_convert_fusion = bf16[768,3072]{1,0:T(8,128)(2,1)} fusion(bf16[384,3072]{1,0:T(8,128)(2,1)S(1)} %copy-done, bf16[768,3072]{1,0:T(8,128)(2,1)} %all-gather.10.cloned.1.call-done, bf16[3072,384]{1,0:T(8,128)(2,1)} %param.25), kind=kOutput, calls=%fused_computation.8 | convolution fusion | flops 3628892160 | bytes 14155776 | tf_op jit(solution)/shard_map/dot_general | solution.py:189
  455.2 1.3 select_reduce_fusion
  461.0 213.4 %reduce-scatter.5.cloned.1.call-done = bf16[24,3072]{1,0:T(8,128)(2,1)} async-done(((bf16[768,3072]{1,0:T(8,128)(2,1)}), bf16[24,3072]{1,0:T(8,128)(2,1)}) %reduce-scatter.5.cloned.1.call-update) | async-done | bytes 147472 | tf_op jit(solution)/shard_map/reduce_scatter | solution.py:190
  674.3 1.1 convert_reduce_fusion.2
  675.7 0.9 multiply_convert_fusion.1
  677.1 4.5 collective-permute-start.1
  681.6 1.9 collective-permute-start
  683.7 5.6 collective-permute-done
  689.3 2.8 collective-permute-start.3
  692.1 1.3 collective-permute-start.2
  693.7 4.0 collective-permute-done.2
  698.4 0.8 fusion.23
  (135 shorter events, 13.2 us)
Async XLA Ops:
  7.2 435.5 %copy-start = (bf16[384,3072]{1,0:T(8,128)(2,1)S(1)}, bf16[384,3072]{1,0:T(8,128)(2,1)}, u32[]{:S(2)}) copy-start(bf16[384,3072]{1,0:T(8,128)(2,1)} %param.26) | copy-start | bytes 7077892
  7.2 96.9 %all-gather.6.cloned.1.call-start = ((), (), s32[]{:S(2)}) async-start(), calls=%async_computation.2 | async-start | bytes 7299072 | tf_op jit(solution)/shard_map/all_gather | solution.py:155
  9.0 127.1 %all-gather.8.cloned.1.call-start = ((), (), s32[]{:S(2)}) async-start(), calls=%async_computation.3 | async-start | bytes 21233664 | tf_op jit(solution)/shard_map/all_gather | solution.py:156
  104.1 1.6 copy-start.8
  104.1 161.4 %all-gather.12.cloned.1.call-start = ((), (), s32[]{:S(2)}) async-start(), calls=%async_computation.7 | async-start | bytes 12976128 | tf_op jit(solution)/shard_map/all_gather | solution.py:166
  143.1 2.6 copy-start.28
  143.1 3.2 copy-start.20
  145.7 209.6 %reduce-scatter.3.cloned.1.call-start = ((), (), s32[]{:S(2)}) async-start(), calls=%async_computation.4 | async-start | bytes 1474560 | tf_op jit(solution)/shard_map/reduce_scatter | solution.py:175
  150.9 126.5 %copy-start.3 = (f32[3,1,100,768]{2,3,0,1:T(8,128)}, f32[3,1,100,768]{2,3,0,1:T(8,128)S(1)}, u32[]{:S(2)}) copy-start(f32[3,1,100,768]{2,3,0,1:T(8,128)S(1)} %copy.32) | copy-start | bytes 2764804
  295.7 13.0 %copy-start.10 = (f32[96,12]{0,1:T(8,128)S(1)}, f32[96,12]{0,1:T(8,128)}, u32[]{:S(2)}) copy-start(f32[96,12]{0,1:T(8,128)} %copy-done.9) | copy-start | bytes 13828
  295.7 13.0 %copy-start.15 = (f32[96,12]{0,1:T(8,128)S(1)}, f32[96,12]{0,1:T(8,128)}, u32[]{:S(2)}) copy-start(f32[96,12]{0,1:T(8,128)} %add_rsqrt_fusion) | copy-start | bytes 13828
  295.8 13.0 %copy-start.23 = (f32[64]{0:T(128)S(1)}, f32[64]{0:T(128)}, u32[]{:S(2)}) copy-start(f32[64]{0:T(128)} %param.21) | copy-start | bytes 772
  295.8 23.6 %slice-start = ((s8[4915200]{0:T(1024)(128)(4,1)}), s8[720896]{0:T(1024)(128)(4,1)S(1)}, s32[]{:S(2)}) async-start(s8[4915200]{0:T(1024)(128)(4,1)} %bitcast.211), calls=%async_computation.8 | async-start | bytes 1441792
  308.7 10.7 %slice-start.1 = ((s8[4915200]{0:T(1024)(128)(4,1)}), s8[4194304]{0:T(1024)(128)(4,1)S(1)}, s32[]{:S(2)}) async-start(s8[4915200]{0:T(1024)(128)(4,1)} %bitcast.211), calls=%async_computation.9 | async-start | bytes 8388608
  327.7 4.5 copy-start.2
  332.1 23.2 %copy-start.14 = (f32[1,1,3072]{2,1,0:T(1,128)S(1)}, f32[1,1,3072]{2,1,0:T(1,128)}, u32[]{:S(2)}) copy-start(f32[1,1,3072]{2,1,0:T(1,128)} %get-tuple-element.17) | copy-start | bytes 36868
  332.1 24.6 %copy-start.11 = (f32[1,1,3072]{2,1,0:T(1,128)S(1)}, f32[1,1,3072]{2,1,0:T(1,128)}, u32[]{:S(2)}) copy-start(f32[1,1,3072]{2,1,0:T(1,128)} %get-tuple-element.12) | copy-start | bytes 36868
  332.1 24.7 %copy-start.12 = (f32[1,1,3072]{2,1,0:T(1,128)S(1)}, f32[1,1,3072]{2,1,0:T(1,128)}, u32[]{:S(2)}) copy-start(f32[1,1,3072]{2,1,0:T(1,128)} %get-tuple-element.13) | copy-start | bytes 36868
  332.1 110.5 %all-gather.10.cloned.1.call-start = ((), (), s32[]{:S(2)}) async-start(), calls=%async_computation.5 | async-start | bytes 4866048 | tf_op jit(solution)/shard_map/all_gather | solution.py:183
  357.6 316.7 %reduce-scatter.5.cloned.1.call-start = ((), (), s32[]{:S(2)}) async-start(), calls=%async_computation.6 | async-start | bytes 4866048 | tf_op jit(solution)/shard_map/reduce_scatter | solution.py:190
  453.0 6.6 copy-start.22
  453.0 221.3 %copy-start.13 = (f32[1,1,3072]{2,1,0:T(1,128)S(1)}, f32[1,1,3072]{2,1,0:T(1,128)}, u32[]{:S(2)}) copy-start(f32[1,1,3072]{2,1,0:T(1,128)} %get-tuple-element.14) | copy-start | bytes 36868
  453.1 222.6 %copy-start.16 = (f32[1,1,3072]{2,1,0:T(1,128)S(1)}, f32[1,1,3072]{2,1,0:T(1,128)}, u32[]{:S(2)}) copy-start(f32[1,1,3072]{2,1,0:T(1,128)} %get-tuple-element.11) | copy-start | bytes 36868
  453.1 222.6 %copy-start.17 = (f32[1,1,3072]{2,1,0:T(1,128)S(1)}, f32[1,1,3072]{2,1,0:T(1,128)}, u32[]{:S(2)}) copy-start(f32[1,1,3072]{2,1,0:T(1,128)} %get-tuple-element.18) | copy-start | bytes 36868
  453.1 222.6 %copy-start.26 = (bf16[3072,64]{0,1:T(8,128)(2,1)S(1)}, bf16[3072,64]{0,1:T(8,128)(2,1)}, u32[]{:S(2)}) copy-start(bf16[3072,64]{0,1:T(8,128)(2,1)} %param.27) | copy-start | bytes 1179652
  453.1 222.6 %copy-start.27 = (f32[1,24,64]{2,1,0:T(8,128)S(1)}, f32[1,24,64]{2,1,0:T(8,128)}, u32[]{:S(2)}) copy-start(f32[1,24,64]{2,1,0:T(8,128)} %param.28) | copy-start | bytes 18436
  453.1 230.4 %copy-start.7 = (bf16[3,3,16,512]{3,2,1,0:T(8,128)(2,1)S(1)}, bf16[3,3,16,512]{3,2,1,0:T(8,128)(2,1)}, u32[]{:S(2)}) copy-start(bf16[3,3,16,512]{3,2,1,0:T(8,128)(2,1)} %param.29) | copy-start | bytes 442372
  675.4 23.8 %copy-start.5 = (bf16[24,3072]{1,0:T(8,128)(2,1)}, bf16[24,3072]{1,0:T(8,128)(2,1)S(1)}, u32[]{:S(2)}) copy-start(bf16[24,3072]{1,0:T(8,128)(2,1)S(1)} %get-tuple-element.8) | copy-start | bytes 442372
  677.1 6.6 collective-permute-start.1
  681.6 7.7 %collective-permute-start = (bf16[6,1,8,16]{3,2,1,0:T(8,128)(2,1)S(1)}, bf16[6,1,8,16]{3,2,1,0:T(8,128)(2,1)S(1)}, u32[]{:S(2)}, u32[]{:S(2)}) collective-permute-start(bf16[6,1,8,16]{3,2,1,0:T(8,128)(2,1)S(1)} %get-tuple-element.21), channel_id=1, source_target_pairs={{0,4},{4,8},{8,12},{12,16},{16,20},{20,24},{24,28},{28,32},{32,36}... | collective-permute-start | bytes 4616 | tf_op jit(solution)/shard_map/ppermute | solution.py:23
  689.3 8.7 %collective-permute-start.3 = (bf16[6,4,1,16]{3,2,1,0:T(2,128)(2,1)S(1)}, bf16[6,4,1,16]{3,2,1,0:T(2,128)(2,1)S(1)}, u32[]{:S(2)}, u32[]{:S(2)}) collective-permute-start(bf16[6,4,1,16]{3,2,1,0:T(2,128)(2,1)S(1)} %get-tuple-element.20), channel_id=1, source_target_pairs={{1,0},{2,1},{3,2},{5,4},{6,5},{7,6},{9,8},{10,9},{11,10},{13,12},{... | collective-permute-start | bytes 2312 | tf_op jit(solution)/shard_map/ppermute | solution.py:25
  692.1 5.6 collective-permute-start.2
  (9 other events, 7.9 us)
Sparse Core Ops, SparseCore 0:
  10.6 93.4 all-gather.5
  105.9 30.1 all-gather.7
  145.8 119.6 all-gather.11
  332.3 22.9 reduce-scatter.2
  358.3 84.3 all-gather.9
  453.3 221.0 reduce-scatter.4
where the time goes:
time: 707 us; the launch traced here: 706 us
  waiting for transfers between devices  567 us (80%)
  local copies, waits for them, and re-layouts  50.3 us (7%)
  matrix products  43.7 us (6%)
  between operations  18.5 us (3%)
  other arithmetic  16 us (2%)
  starting transfers between devices  10.9 us (2%)
    reduce_scatter x1, waiting for transfers between devices, shards(): lax.psum_scatter(feed_terms.astype(jnp.bfloat16), 'row', scatter_dimensio...  213 us
    all_gather x1, waiting for transfers between devices, shards(): both = lax.all_gather(both, 'row', axis=0, tiled=True)  113 us
    all_gather x1, waiting for transfers between devices, shards(): gathered_half = lax.all_gather(own_half, 'row', axis=1, tiled=True)  95 us
    all_gather x1, waiting for transfers between devices, shards(): lax.all_gather(second_norm, 'row', axis=0, tiled=True)  84.8 us
    all_gather x1, waiting for transfers between devices, shards(): lax.all_gather(gathered_half, 'req', axis=2, tiled=True)  28.7 us
    another operation x4, local copies, waits for them, and re-layouts  26 us
    reduce_scatter x1, waiting for transfers between devices, shards(): lax.psum_scatter(partial_out, 'col', scatter_dimension=0, tiled=True)  22 us
  transfers between devices with their start and end apart: 10, of which 8 were waited for; matrix products, arithmetic and copies ran while one was open for 2% of the time, Pallas kernels for 0%

commit v1 on v0

--- a/solution.py
+++ b/solution.py
@@ -10,6 +10,10 @@
 TRAIN_STEPS = 1000
 STRIDE = 250
 latent_scale = 0.7
+_see_local_data = lambda inputs, named_axis: jnp.concatenate(
+    lax.all_to_all(jnp.stack([inputs for _ in range(lax.axis_size(named_axis))]), named_axis, 0, 0),
+    axis=0,
+)
 
 
 def extended(cells, sides, width):
@@ -180,9 +184,7 @@
     second_norm = modulate(mixed, adaptive[3], adaptive[4])
     hidden_units = jax.nn.gelu(
         jnp.dot(
-            lax.all_gather(second_norm, "row", axis=0, tiled=True),
-            w_up,
-            preferred_element_type=jnp.float32,
+            _see_local_data(second_norm, named_axis="row"), w_up, preferred_element_type=jnp.float32
         ),
         approximate=True,
     ).astype(jnp.bfloat16)

time: 707 us -> 736 us (1.041)
  blocking collectives: 0 us -> 115 us
  waiting for transfers between devices: 567 us -> 482 us
    all_to_all x0 -> x1, blocking collectives: none -> 115 us  [lax.all_to_all(jnp.stack([inputs for _ in range(lax.axis_size(named_axis)...]
    all_gather x1 -> x0, waiting for transfers between devices: 84.8 us -> none  [shards(): lax.all_gather(second_norm, 'row', axis=0, tiled=True)]
    another operation x4 -> x5, local copies, waits for them, and re-layouts: 26 us -> 26.5 us
  transfers between devices with their start and end apart: 10 -> 9, of which waited for: 8 -> 7; matrix products, arithmetic and copies ran while one was open for 2% -> 2% of each run, Pallas kernels for 0% -> 0%
where the time goes in v1:
time: 736 us; the launch traced here: 735 us
  waiting for transfers between devices  482 us (65%)
  blocking collectives  115 us (16%)
  local copies, waits for them, and re-layouts  50.3 us (7%)
  matrix products  43.6 us (6%)
  between operations  18.2 us (2%)
  other arithmetic  15.4 us (2%)
  starting transfers between devices  11 us (1%)
    reduce_scatter x1, waiting for transfers between devices, shards(): lax.psum_scatter(feed_terms.astype(jnp.bfloat16), 'row', scatter_dimensio...  213 us
    all_to_all x1, blocking collectives, lax.all_to_all(jnp.stack([inputs for _ in range(lax.axis_size(named_axis)...  115 us
    all_gather x1, waiting for transfers between devices, shards(): both = lax.all_gather(both, 'row', axis=0, tiled=True)  113 us
    all_gather x1, waiting for transfers between devices, shards(): gathered_half = lax.all_gather(own_half, 'row', axis=1, tiled=True)  95 us
    all_gather x1, waiting for transfers between devices, shards(): lax.all_gather(gathered_half, 'req', axis=2, tiled=True)  29.3 us
    another operation x4, local copies, waits for them, and re-layouts  26 us
    reduce_scatter x1, waiting for transfers between devices, shards(): lax.psum_scatter(partial_out, 'col', scatter_dimension=0, tiled=True)  21.7 us
  transfers between devices with their start and end apart: 9, of which 7 were waited for; matrix products, arithmetic and copies ran while one was open for 2% of the time, Pallas kernels for 0%

profile of v1, /device:TPU:26, one launch (start us, length us, event | category | flops | bytes accessed | tf_op | source)
XLA Modules:
  0.0 734.9 jit_solution(14316434215863838945)
XLA Ops:
  7.3 1.8 constant_dynamic-slice_fusion
  9.1 95.0 %all-gather.5.cloned.1.call-done = bf16[3,3072,384]{2,1,0:T(8,128)(2,1)} async-done(((bf16[3,96,384]{2,1,0:T(8,128)(2,1)}), bf16[3,3072,384]{2,1,0:T(8,128)(2,1)}) %all-gather.5.cloned.1.call-update) | async-done | bytes 7077904 | tf_op jit(solution)/shard_map/all_gather | solution.py:159
  106.8 29.3 %all-gather.7.cloned.1.call-done = bf16[3,3072,768]{2,1,0:T(8,128)(2,1)} async-done(((bf16[3,3072,384]{2,1,0:T(8,128)(2,1)}), bf16[3,3072,768]{2,1,0:T(8,128)(2,1)}) %all-gather.7.cloned.1.call-update) | async-done | bytes 14155792 | tf_op jit(solution)/shard_map/all_gather | solution.py:160
  136.1 7.0 convolution_bitcast_fusion
  143.2 1.0 copy-done.4
  144.8 0.8 pad_maximum_fusion
  147.3 2.0 fusion.152
  149.3 1.6 copy.32
  152.3 113.2 %all-gather.9.cloned.1.call-done = bf16[64,100,12,64]{1,3,2,0:T(8,128)(2,1)} async-done(((bf16[2,100,12,64]{1,3,2,0:T(8,128)(2,1)}), bf16[64,100,12,64]{1,3,2,0:T(8,128)(2,1)}) %all-gather.9.cloned.1.call-update) | async-done | bytes 9830416 | tf_op jit(solution)/shard_map/all_gather | solution.py:170
  265.5 11.9 %copy.45 = bf16[32,2,100,12,64]{2,0,4,3,1:T(8,128)(2,1)S(1)} copy(bf16[32,2,100,12,64]{2,4,3,1,0:T(8,128)(2,1)} %bitcast.214) | data formatting | bytes 19660800 | tf_op jit(solution)/shard_map/all_gather | solution.py:170
  277.4 5.5 fusion.175
  282.9 12.9 %reshape.418 = bf16[3200,12,64]{0,2,1:T(8,128)(2,1)} reshape(bf16[1,32,100,12,64]{2,1,4,3,0:T(8,128)(2,1)} %get-tuple-element.10) | data formatting | bytes 9830400 | tf_op jit(solution)/shard_map/reshape.46
  295.8 13.0 %reshape.419 = bf16[3200,12,64]{0,2,1:T(8,128)(2,1)} reshape(bf16[1,32,100,12,64]{2,1,4,3,0:T(8,128)(2,1)} %get-tuple-element.9) | data formatting | bytes 9830400 | tf_op jit(solution)/shard_map/reshape.38
  308.8 10.7 %bitcast_reduce_fusion = (f32[96,12]{0,1:T(8,128)S(1)}, f32[12,3200,96]{1,2,0:T(8,128)}) fusion(f32[3200]{0:T(1024)S(1)} %fusion.152, bf16[3200,12,64]{0,2,1:T(8,128)(2,1)} %reshape.419, f32[3,1,100,12,64]{2,4,3,0,1:T(8,128)} %bitcast.221, f32[64]{0:T(128)S(1)} %copy-done.23, f32[96,12]{0,1:T(8,128)S(1)} %copy-done.15, f32[96,12]{0,1:T(8,128)S(1)} %copy-done.10), kind=kOutput, calls=%fused_computation | convolution fusion | flops 483212160 | bytes 20080896 | tf_op jit(solution)/shard_map/gqhd,gkhd->gqhk/dot_general | solution.py:105
  319.4 8.3 %fusion.29 = bf16[1,96,12,64]{1,3,2,0:T(8,128)(2,1)S(1)} fusion(bf16[3200,12,64]{0,2,1:T(8,128)(2,1)S(1)} %bitcast.213, f32[12,3200,96]{1,2,0:T(8,128)} %get-tuple-element.24, f32[3200]{0:T(1024)S(1)} %fusion.152, f32[96,12]{0,1:T(8,128)S(1)} %get-tuple-element.23), kind=kOutput, calls=%fused_computation.37 | convolution fusion | flops 483065856 | bytes 19825664 | tf_op jit(solution)/shard_map/gqhk,gkhd->gqhd/dot_general | solution.py:109
  327.8 4.4 fusion.179
  332.5 1.1 convert_element_type.114
  333.6 21.7 %reduce-scatter.3.cloned.1.call-done = f32[24,3072]{1,0:T(8,128)} async-done(((f32[96,3072]{1,0:T(8,128)}), f32[24,3072]{1,0:T(8,128)}) %reduce-scatter.3.cloned.1.call-update) | async-done | bytes 294928 | tf_op jit(solution)/shard_map/reduce_scatter | solution.py:179
  355.3 1.1 fusion.57
  357.5 114.9 %all_to_all.5 = bf16[32,24,3072]{2,1,0:T(8,128)(2,1)} all-to-all(bf16[32,24,3072]{2,1,0:T(8,128)(2,1)S(1)} %stack.5), channel_id=1, replica_groups=mesh['req'=2,'row'=32,'col'=4] {'row'}, dimensions={0} | all-to-all | bytes 9437184 | tf_op jit(solution)/shard_map/all_to_all | solution.py:14
  472.4 10.4 %convolution_convert_fusion = bf16[768,3072]{1,0:T(8,128)(2,1)} fusion(bf16[384,3072]{1,0:T(8,128)(2,1)S(1)} %copy-done, bf16[768,3072]{1,0:T(8,128)(2,1)} %bitcast.218, bf16[3072,384]{1,0:T(8,128)(2,1)} %param.25), kind=kOutput, calls=%fused_computation.8 | convolution fusion | flops 3628892160 | bytes 14155776 | tf_op jit(solution)/shard_map/dot_general | solution.py:191
  484.9 1.3 select_reduce_fusion
  490.7 212.6 %reduce-scatter.5.cloned.1.call-done = bf16[24,3072]{1,0:T(8,128)(2,1)} async-done(((bf16[768,3072]{1,0:T(8,128)(2,1)}), bf16[24,3072]{1,0:T(8,128)(2,1)}) %reduce-scatter.5.cloned.1.call-update) | async-done | bytes 147472 | tf_op jit(solution)/shard_map/reduce_scatter | solution.py:192
  703.3 1.1 convert_reduce_fusion.2
  704.7 0.9 multiply_convert_fusion.1
  706.1 4.6 collective-permute-start.1
  710.7 1.9 collective-permute-start
  712.8 5.6 collective-permute-done
  718.4 2.8 collective-permute-start.3
  721.2 1.3 collective-permute-start.2
  722.8 4.0 collective-permute-done.2
  727.6 0.8 fusion.23
  (134 shorter events, 12.4 us)
Async XLA Ops:
  7.2 465.2 %copy-start = (bf16[384,3072]{1,0:T(8,128)(2,1)S(1)}, bf16[384,3072]{1,0:T(8,128)(2,1)}, u32[]{:S(2)}) copy-start(bf16[384,3072]{1,0:T(8,128)(2,1)} %param.26) | copy-start | bytes 7077892
  7.2 97.0 %copy-start.6 = (bf16[1,4,3072]{2,1,0:T(4,128)(2,1)S(1)}, bf16[1,4,3072]{2,1,0:T(4,128)(2,1)}, u32[]{:S(2)}) copy-start(bf16[1,4,3072]{2,1,0:T(4,128)(2,1)} %param.16) | copy-start | bytes 73732
  7.2 97.4 %copy-start.1 = (bf16[1,96,3072]{2,1,0:T(8,128)(2,1)S(1)}, bf16[1,96,3072]{2,1,0:T(8,128)(2,1)}, u32[]{:S(2)}) copy-start(bf16[1,96,3072]{2,1,0:T(8,128)(2,1)} %param.15) | copy-start | bytes 1769476
  7.2 97.9 %copy-start.8 = (f32[1,8,3072]{2,1,0:T(8,128)S(1)}, f32[1,8,3072]{2,1,0:T(8,128)}, u32[]{:S(2)}) copy-start(f32[1,8,3072]{2,1,0:T(8,128)} %param.20) | copy-start | bytes 294916
  7.2 96.9 %all-gather.5.cloned.1.call-start = ((), (), s32[]{:S(2)}) async-start(), calls=%async_computation.3 | async-start | bytes 7299072 | tf_op jit(solution)/shard_map/all_gather | solution.py:159
  9.1 127.1 %all-gather.7.cloned.1.call-start = ((), (), s32[]{:S(2)}) async-start(), calls=%async_computation.4 | async-start | bytes 21233664 | tf_op jit(solution)/shard_map/all_gather | solution.py:160
  104.1 161.4 %all-gather.9.cloned.1.call-start = ((), (), s32[]{:S(2)}) async-start(), calls=%async_computation.7 | async-start | bytes 12976128 | tf_op jit(solution)/shard_map/all_gather | solution.py:170
  106.8 37.9 %copy-start.25 = (f32[64]{0:T(128)S(1)}, f32[64]{0:T(128)}, u32[]{:S(2)}) copy-start(f32[64]{0:T(128)} %param.22) | copy-start | bytes 772
  106.8 39.0 %copy-start.28 = (s32[2]{0:T(128)S(1)}, s32[2]{0:T(128)}, u32[]{:S(2)}) copy-start(s32[2]{0:T(128)} %param.17) | copy-start | bytes 28
  106.8 39.6 %copy-start.20 = (s32[2,2]{1,0:T(2,128)S(1)}, s32[2,2]{1,0:T(2,128)}, u32[]{:S(2)}) copy-start(s32[2,2]{1,0:T(2,128)} %param.18) | copy-start | bytes 52
  145.7 209.6 %reduce-scatter.3.cloned.1.call-start = ((), (), s32[]{:S(2)}) async-start(), calls=%async_computation.5 | async-start | bytes 1474560 | tf_op jit(solution)/shard_map/reduce_scatter | solution.py:179
  150.9 126.5 %copy-start.3 = (f32[3,1,100,768]{2,3,0,1:T(8,128)}, f32[3,1,100,768]{2,3,0,1:T(8,128)S(1)}, u32[]{:S(2)}) copy-start(f32[3,1,100,768]{2,3,0,1:T(8,128)S(1)} %copy.32) | copy-start | bytes 2764804
  295.8 13.0 %copy-start.10 = (f32[96,12]{0,1:T(8,128)S(1)}, f32[96,12]{0,1:T(8,128)}, u32[]{:S(2)}) copy-start(f32[96,12]{0,1:T(8,128)} %copy-done.9) | copy-start | bytes 13828
  295.8 13.0 %copy-start.15 = (f32[96,12]{0,1:T(8,128)S(1)}, f32[96,12]{0,1:T(8,128)}, u32[]{:S(2)}) copy-start(f32[96,12]{0,1:T(8,128)} %add_rsqrt_fusion) | copy-start | bytes 13828
  295.8 13.0 %copy-start.23 = (f32[64]{0:T(128)S(1)}, f32[64]{0:T(128)}, u32[]{:S(2)}) copy-start(f32[64]{0:T(128)} %param.21) | copy-start | bytes 772
  295.8 23.6 %slice-start = ((s8[4915200]{0:T(1024)(128)(4,1)}), s8[720896]{0:T(1024)(128)(4,1)S(1)}, s32[]{:S(2)}) async-start(s8[4915200]{0:T(1024)(128)(4,1)} %bitcast.212), calls=%async_computation.8 | async-start | bytes 1441792
  308.8 10.7 %slice-start.1 = ((s8[4915200]{0:T(1024)(128)(4,1)}), s8[4194304]{0:T(1024)(128)(4,1)S(1)}, s32[]{:S(2)}) async-start(s8[4915200]{0:T(1024)(128)(4,1)} %bitcast.212), calls=%async_computation.9 | async-start | bytes 8388608
  327.8 27.5 %copy-start.14 = (f32[1,1,3072]{2,1,0:T(1,128)S(1)}, f32[1,1,3072]{2,1,0:T(1,128)}, u32[]{:S(2)}) copy-start(f32[1,1,3072]{2,1,0:T(1,128)} %get-tuple-element.17) | copy-start | bytes 36868
  327.8 29.0 %copy-start.11 = (f32[1,1,3072]{2,1,0:T(1,128)S(1)}, f32[1,1,3072]{2,1,0:T(1,128)}, u32[]{:S(2)}) copy-start(f32[1,1,3072]{2,1,0:T(1,128)} %get-tuple-element.12) | copy-start | bytes 36868
  327.8 29.0 %copy-start.12 = (f32[1,1,3072]{2,1,0:T(1,128)S(1)}, f32[1,1,3072]{2,1,0:T(1,128)}, u32[]{:S(2)}) copy-start(f32[1,1,3072]{2,1,0:T(1,128)} %get-tuple-element.13) | copy-start | bytes 36868
  332.2 371.1 %reduce-scatter.5.cloned.1.call-start = ((), (), s32[]{:S(2)}) async-start(), calls=%async_computation.6 | async-start | bytes 4866048 | tf_op jit(solution)/shard_map/reduce_scatter | solution.py:192
  482.8 220.6 %copy-start.13 = (f32[1,1,3072]{2,1,0:T(1,128)S(1)}, f32[1,1,3072]{2,1,0:T(1,128)}, u32[]{:S(2)}) copy-start(f32[1,1,3072]{2,1,0:T(1,128)} %get-tuple-element.14) | copy-start | bytes 36868
  482.8 221.9 %copy-start.16 = (f32[1,1,3072]{2,1,0:T(1,128)S(1)}, f32[1,1,3072]{2,1,0:T(1,128)}, u32[]{:S(2)}) copy-start(f32[1,1,3072]{2,1,0:T(1,128)} %get-tuple-element.11) | copy-start | bytes 36868
  482.8 221.9 %copy-start.17 = (f32[1,1,3072]{2,1,0:T(1,128)S(1)}, f32[1,1,3072]{2,1,0:T(1,128)}, u32[]{:S(2)}) copy-start(f32[1,1,3072]{2,1,0:T(1,128)} %get-tuple-element.18) | copy-start | bytes 36868
  482.8 221.9 %copy-start.26 = (bf16[3072,64]{0,1:T(8,128)(2,1)S(1)}, bf16[3072,64]{0,1:T(8,128)(2,1)}, u32[]{:S(2)}) copy-start(bf16[3072,64]{0,1:T(8,128)(2,1)} %param.27) | copy-start | bytes 1179652
  482.8 221.9 %copy-start.27 = (f32[1,24,64]{2,1,0:T(8,128)S(1)}, f32[1,24,64]{2,1,0:T(8,128)}, u32[]{:S(2)}) copy-start(f32[1,24,64]{2,1,0:T(8,128)} %param.28) | copy-start | bytes 18436
  482.8 229.8 %copy-start.7 = (bf16[3,3,16,512]{3,2,1,0:T(8,128)(2,1)S(1)}, bf16[3,3,16,512]{3,2,1,0:T(8,128)(2,1)}, u32[]{:S(2)}) copy-start(bf16[3,3,16,512]{3,2,1,0:T(8,128)(2,1)} %param.29) | copy-start | bytes 442372
  704.4 24.0 %copy-start.5 = (bf16[24,3072]{1,0:T(8,128)(2,1)}, bf16[24,3072]{1,0:T(8,128)(2,1)S(1)}, u32[]{:S(2)}) copy-start(bf16[24,3072]{1,0:T(8,128)(2,1)S(1)} %get-tuple-element.8) | copy-start | bytes 442372
  706.1 6.7 collective-permute-start.1
  710.7 7.7 %collective-permute-start = (bf16[6,1,8,16]{3,2,1,0:T(8,128)(2,1)S(1)}, bf16[6,1,8,16]{3,2,1,0:T(8,128)(2,1)S(1)}, u32[]{:S(2)}, u32[]{:S(2)}) collective-permute-start(bf16[6,1,8,16]{3,2,1,0:T(8,128)(2,1)S(1)} %get-tuple-element.21), channel_id=1, source_target_pairs={{0,4},{4,8},{8,12},{12,16},{16,20},{20,24},{24,28},{28,32},{32,36}... | collective-permute-start | bytes 4616 | tf_op jit(solution)/shard_map/ppermute | solution.py:27
  718.4 8.7 %collective-permute-start.3 = (bf16[6,4,1,16]{3,2,1,0:T(2,128)(2,1)S(1)}, bf16[6,4,1,16]{3,2,1,0:T(2,128)(2,1)S(1)}, u32[]{:S(2)}, u32[]{:S(2)}) collective-permute-start(bf16[6,4,1,16]{3,2,1,0:T(2,128)(2,1)S(1)} %get-tuple-element.20), channel_id=1, source_target_pairs={{1,0},{2,1},{3,2},{5,4},{6,5},{7,6},{9,8},{10,9},{11,10},{13,12},{... | collective-permute-start | bytes 2312 | tf_op jit(solution)/shard_map/ppermute | solution.py:29
  721.2 5.6 collective-permute-start.2
  (8 other events, 15.8 us)
Sparse Core Ops, SparseCore 0:
  10.6 93.4 all-gather.4
  105.9 30.1 all-gather.6
  145.8 119.6 all-gather.8
  332.3 22.9 reduce-scatter.2
  483.0 220.3 reduce-scatter.4
